TPU v7x, 512 devices: a whole 4x8x8 slice. The times are simulated.
512 devices in a mesh: region: 8 (over x, core), owner: 64 (over y, z).
Axes of the slice: x: 4, y: 8, z: 8, core: 2. Of those that a mesh axis runs over, the one named last changes fastest.
Arguments:
- voxels: bfloat16 [8, 64, 1, 256, 1024], P('region', 'owner'), may hold values from -6 to 6
- norm_gain: float32 [1024], replicated, may hold values from 0.5 to 1.5
- qkv_weight: bfloat16 [1024, 3072], P(('region', 'owner')), may hold values from -0.14453125 to 0.14453125
- out_weight: bfloat16 [1024, 1024], P(('region', 'owner')), may hold values from -0.1875 to 0.1875
- neighbours: int32 [8, 64, 1, 8], P('region', 'owner'), may hold values from -1 to 511, as said below
Outputs:
- attended_voxels: bfloat16 [8, 64, 1, 256, 1024], P('region', 'owner')
Inputs may be any that keep to these rules, and one draw needn't show every extreme that they name: `neighbours`: each entry is -1 or the number (r * 64 + o) + c of a block c held by the device at region r and owner o, where r and o each differ by at most one from those of the list's own block; a list never names its own block and names no block twice.
All inputs are finite; a program needn't handle non-finite values.
Results may differ from a plain program's by a relative error of at most 0.0057.
Values may be sent and summed in bfloat16 or wider, within the bound.
No kernel may reach another device: no remote copies, remote signals or barrier semaphores. Data moves between devices by JAX's collectives and lax.ppermute only.
A program may use at most 64 MiB of HBM per device.

v0:
```python
import jax
import jax.numpy as jnp
from jax import lax
from jax.sharding import PartitionSpec as P

HEAD_DIM = 64


def in_order(blocks, dim):
    shape = list(blocks.shape[1:])
    shape[dim] *= blocks.shape[0]
    return jnp.moveaxis(blocks, 0, dim).reshape(shape)


def from_everyone(value, axis):
    devices = lax.axis_size(axis)
    return lax.all_to_all(
        jnp.broadcast_to(value[None], (devices, *value.shape)), axis, 0, 0, tiled=True
    )


def gathered_copies(value, axis, dim):
    return in_order(from_everyone(value, axis), dim)


def padded(value, sides, width):
    for axis, dim in sides:
        devices, length = (lax.axis_size(axis), value.shape[dim])
        up = [(i, (i + 1) % devices) for i in range(devices - 1)]
        down = [(j, i) for i, j in up]
        last = lax.slice_in_dim(value, length - width, length, axis=dim)
        first = lax.slice_in_dim(value, 0, width, axis=dim)
        before = lax.ppermute(last, axis, up)
        after = lax.ppermute(first, axis, down)
        value = jnp.concatenate([before, value, after], axis=dim)
    return value


def layer_norm(inputs, norm_gain):
    widened = inputs.astype(jnp.float32)
    average = jnp.mean(widened, axis=-1, keepdims=True)
    spread = jnp.mean((widened - average) ** 2, axis=-1, keepdims=True)
    return ((widened - average) * lax.rsqrt(spread + 1e-06) * norm_gain).astype(jnp.bfloat16)


def shards(voxels, norm_gain, qkv_weight, out_weight, neighbours):
    capacity = voxels.shape[2]
    block_size = voxels.shape[3]
    model_width = voxels.shape[4]
    token_count = capacity * block_size
    flat_tokens = voxels.reshape(token_count, model_width)
    normed = layer_norm(flat_tokens, norm_gain)
    group_rows = gathered_copies(qkv_weight, "owner", 0)
    columns = normed
    qkv = jnp.dot(
        columns,
        lax.all_gather(group_rows, "region", axis=0, tiled=True),
        preferred_element_type=jnp.float32,
    )
    qkv = qkv.astype(jnp.bfloat16)
    queries = qkv[:, :model_width].reshape(capacity, block_size, model_width)
    kv_pairs = qkv[:, model_width:].reshape(1, 1, capacity, block_size, 2 * model_width)
    extended = padded(kv_pairs, (("region", 0), ("owner", 1)), 1)
    extended = extended.reshape(9 * capacity * block_size, 2 * model_width)
    key_rows = extended[:, :model_width]
    value_rows = extended[:, model_width:]
    owner_count = lax.axis_size("owner")
    my_region = lax.axis_index("region")
    my_owner = lax.axis_index("owner")
    list_ids = neighbours.reshape(capacity, neighbours.shape[-1])
    far_region = list_ids // (owner_count * capacity)
    far_owner = list_ids // capacity % owner_count
    far_slot = list_ids % capacity
    local_ids = (
        (far_region - my_region + 1) * 3 + (far_owner - my_owner + 1)
    ) * capacity + far_slot
    local_ids = jnp.where(list_ids >= 0, local_ids, -1)
    slot_ids = jnp.arange(9 * capacity, dtype=jnp.int32)
    listed = jnp.any(local_ids[:, :, None] == slot_ids[None, None, :], axis=1)
    own_block = slot_ids[None, :] == (4 * capacity + jnp.arange(capacity, dtype=jnp.int32))[:, None]
    allowed = listed | own_block
    key_mask = jnp.repeat(allowed, block_size, axis=1)
    group_heads = 2
    group_cols = group_heads * HEAD_DIM
    group_count = model_width // group_cols
    score_scale = HEAD_DIM ** (-0.5)

    def attend_group(group_idx, buffer):
        offset = group_idx * group_cols
        query_part = lax.dynamic_slice_in_dim(queries, offset, group_cols, 2).reshape(
            capacity, block_size, group_heads, HEAD_DIM
        )
        key_part = lax.dynamic_slice_in_dim(key_rows, offset, group_cols, 1).reshape(
            -1, group_heads, HEAD_DIM
        )
        value_part = lax.dynamic_slice_in_dim(value_rows, offset, group_cols, 1).reshape(
            -1, group_heads, HEAD_DIM
        )
        scores = (
            jnp.einsum("cshd,khd->chsk", query_part, key_part, preferred_element_type=jnp.float32)
            * score_scale
        )
        scores = jnp.where(key_mask[:, None, None, :], scores, -1e30)
        row_max = jnp.max(scores, axis=-1, keepdims=True)
        shifted = jnp.exp(scores - row_max)
        attn_probs = (shifted / jnp.sum(shifted, axis=-1, keepdims=True)).astype(jnp.bfloat16)
        attended = jnp.einsum(
            "chsk,khd->cshd", attn_probs, value_part, preferred_element_type=jnp.float32
        )
        attended = attended.astype(jnp.bfloat16).reshape(capacity, block_size, group_cols)
        return lax.dynamic_update_slice_in_dim(buffer, attended, offset, 2)

    mixed = lax.fori_loop(
        0, group_count, attend_group, jnp.zeros((capacity, block_size, model_width), jnp.bfloat16)
    )
    mixed_rows = mixed.reshape(token_count, model_width)
    columns = mixed_rows
    projected = jnp.dot(
        columns,
        lax.all_gather(out_weight, ("region", "owner"), axis=0, tiled=True),
        preferred_element_type=jnp.float32,
    )
    result = flat_tokens.astype(jnp.float32) + projected
    return result.astype(jnp.bfloat16).reshape(voxels.shape)


def solution(mesh):
    return jax.shard_map(
        shards,
        mesh=mesh,
        in_specs=(
            P("region", "owner", None, None, None),
            P(),
            P(("region", "owner"), None),
            P(("region", "owner"), None),
            P("region", "owner", None, None),
        ),
        out_specs=P("region", "owner", None, None, None),
        check_vma=False,
    )
```

profile of v0, /device:TPU:1, one launch (start us, length us, event | category | flops | bytes accessed | tf_op | source)
XLA Modules:
  0.0 356.1 jit_solution(15957770580684786674)
XLA Ops:
  8.5 38.6 %all_to_all.5 = bf16[64,2,3072]{2,1,0:T(2,128)(2,1)S(1)} all-to-all(bf16[64,2,3072]{2,1,0:T(2,128)(2,1)S(1)} %broadcast_in_dim.53), channel_id=1, replica_groups=mesh['region'=8,'owner'=64] {'owner'}, dimensions={0} | all-to-all | bytes 1572864 | tf_op jit(solution)/shard_map/all_to_all | solution.py:17
  48.9 43.2 %all-gather.4.cloned.1.call-done = bf16[1024,3072]{1,0:T(8,128)(2,1)} async-done(((bf16[128,3072]{1,0:T(8,128)(2,1)}), bf16[1024,3072]{1,0:T(8,128)(2,1)}) %all-gather.4.cloned.1.call-update) | async-done | bytes 6291472 | tf_op jit(solution)/shard_map/all_gather | solution.py:57
  92.1 4.7 %convolution_convert_fusion = bf16[256,3072]{1,0:T(8,128)(2,1)S(1)} fusion(bf16[1024,3072]{1,0:T(8,128)(2,1)} %all-gather.4.cloned.1.call-done, bf16[1,1,1,256,1024]{4,3,2,1,0:T(8,128)(2,1)S(1)} %copy-done.2, f32[1024]{0:T(1024)S(1)} %copy-done.8, f32[256]{0:T(256)S(1)} %add_rsqrt_fusion, f32[256]{0:T(256)S(1)} %broadcast_multiply_fusion), kind=kOutput, calls=%fused_computation.17 | convolution fusion | flops 1612709888 | bytes 8394752 | tf_op jit(solution)/shard_map/dot_general | solution.py:55
  98.0 2.4 collective-permute-start
  102.4 9.7 %collective-permute-done = bf16[1,1,1,256,2048]{4,3,2,1,0:T(8,128)(2,1)S(1)} collective-permute-done((bf16[1,1,1,256,2048]{4,3,2,1,0:T(8,128)(2,1)S(1)}, bf16[1,1,1,256,2048]{4,3,2,1,0:T(8,128)(2,1)S(1)}, u32[]{:S(2)}, u32[]{:S(2)}) %collective-permute-start) | collective-permute-done | bytes 1048608 | tf_op jit(solution)/shard_map/ppermute | solution.py:33
  112.1 4.4 %collective-permute-done.1 = bf16[1,1,1,256,2048]{4,3,2,1,0:T(8,128)(2,1)S(1)} collective-permute-done((bf16[1,1,1,256,2048]{4,3,2,1,0:T(8,128)(2,1)S(1)}, bf16[1,1,1,256,2048]{4,3,2,1,0:T(8,128)(2,1)S(1)}, u32[]{:S(2)}, u32[]{:S(2)}) %collective-permute-start.1) | collective-permute-done | bytes 1048608 | tf_op jit(solution)/shard_map/ppermute | solution.py:34
  118.5 5.4 %collective-permute-start.2 = (bf16[3,1,1,256,2048]{4,3,2,1,0:T(8,128)(2,1)}, bf16[3,1,1,256,2048]{4,3,2,1,0:T(8,128)(2,1)}, u32[]{:S(2)}, u32[]{:S(2)}) collective-permute-start(bf16[3,1,1,256,2048]{4,3,2,1,0:T(8,128)(2,1)} %pad_maximum_fusion.1), channel_id=1, source_target_pairs={{0,1},{1,2},{2,3},{3,4},{4,5},{5,6},{6,7},{7,8},{8,9},{9,10},{10,1... | collective-permute-start | bytes 9437192 | tf_op jit(solution)/shard_map/ppermute | solution.py:33
  125.3 118.2 %all-gather.6.cloned.1.call-done = bf16[512,2,1024]{2,1,0:T(2,128)(2,1)} async-done(((bf16[1,2,1024]{2,1,0:T(2,128)(2,1)}), bf16[512,2,1024]{2,1,0:T(2,128)(2,1)}) %all-gather.6.cloned.1.call-update) | async-done | bytes 2097168 | tf_op jit(solution)/shard_map/all_gather | solution.py:120
  243.5 4.1 %reshape.300 = bf16[1024,1024]{1,0:T(8,128)(2,1)} reshape(bf16[512,2,1024]{2,1,0:T(2,128)(2,1)} %all-gather.6.cloned.1.call-done) | data formatting | bytes 4194304
  249.5 4.7 %pad_maximum_fusion = bf16[3,3,1,256,2048]{4,3,2,1,0:T(8,128)(2,1)S(1)} fusion(bf16[3,1,1,256,2048]{4,3,2,1,0:T(8,128)(2,1)} %collective-permute-done.3, bf16[1,1,1,256,2048]{4,3,2,1,0:T(8,128)(2,1)} %copy-done.5, bf16[1,1,1,256,2048]{4,3,2,1,0:T(8,128)(2,1)} %copy-done.1, bf16[1,1,1,256,2048]{4,3,2,1,0:T(8,128)(2,1)} %copy-done.4, ...), kind=kLoop, calls=%fused_computation.16 | loop fusion | flops 18874368 | bytes 18874368 | tf_op jit(solution)/shard_map/concatenate | solution.py:35
  254.2 4.8 %fusion.28 = (bf16[2304,1024]{1,0:T(8,128)(2,1)}, bf16[2304,1024]{1,0:T(8,128)(2,1)}) fusion(bf16[2304,2048]{1,0:T(8,128)(2,1)S(1)} %bitcast.105), kind=kLoop, calls=%fused_computation.51 | loop fusion | bytes 18874368 | tf_op jit(solution)/shard_map/slice | solution.py:65
  259.0 86.5 %while.14 = (s32[]{:T(128)}, bf16[1,256,1024]{1,2,0:T(8,128)(2,1)S(1)}, bf16[2304,1024]{1,0:T(8,128)(2,1)}, bf16[2304,1024]{1,0:T(8,128)(2,1)}, bf16[1,256,1024]...) while((s32[]{:T(128)}, ...), condition=%wide.region_6.7_spmd.clone, body=%wide.region_3.6_spmd.clone.sunk | while | flops 311458816 | bytes 39472324 | solution.py:113
  263.5 2.2 copy-done
  266.6 3.3 fusion.45
  274.3 2.2 copy-done
  277.4 3.3 fusion.45
  285.1 2.2 copy-done
  288.2 3.3 fusion.45
  299.0 3.3 fusion.45
  309.8 3.3 fusion.45
  320.6 3.3 fusion.45
  331.4 3.3 fusion.45
  342.2 3.3 fusion.45
  345.5 3.1 fusion.15
  (130 shorter events, 64.7 us)
Async XLA Ops:
  7.4 41.1 %copy-start.2 = (bf16[1,1,1,256,1024]{4,3,2,1,0:T(8,128)(2,1)S(1)}, bf16[1,1,1,256,1024]{4,3,2,1,0:T(8,128)(2,1)}, u32[]{:S(2)}) copy-start(bf16[1,1,1,256,1024]{4,3,2,1,0:T(8,128)(2,1)} %param.7) | copy-start | bytes 1572868
  7.4 84.7 %copy-start.8 = (f32[1024]{0:T(1024)S(1)}, f32[1024]{0:T(1024)}, u32[]{:S(2)}) copy-start(f32[1024]{0:T(1024)} %param.8) | copy-start | bytes 12292
  7.4 84.7 %all-gather.4.cloned.1.call-start = ((), (), s32[]{:S(2)}) async-start(), calls=%async_computation.1 | async-start | bytes 7077888 | tf_op jit(solution)/shard_map/all_gather | solution.py:57
  48.4 195.1 %all-gather.6.cloned.1.call-start = ((), (), s32[]{:S(2)}) async-start(), calls=%async_computation.2 | async-start | bytes 2101248 | tf_op jit(solution)/shard_map/all_gather | solution.py:120
  96.8 1.2 copy-start.6
  96.8 28.4 %copy-start.7 = (s32[1,1,1,8]{3,2,1,0:T(1,128)S(1)}, s32[1,1,1,8]{3,2,1,0:T(1,128)}, u32[]{:S(2)}) copy-start(s32[1,1,1,8]{3,2,1,0:T(1,128)} %param.11) | copy-start | bytes 100
  98.0 149.6 %copy-start.1 = (bf16[1,1,1,256,2048]{4,3,2,1,0:T(8,128)(2,1)}, bf16[1,1,1,256,2048]{4,3,2,1,0:T(8,128)(2,1)S(1)}, u32[]{:S(2)}) copy-start(bf16[1,1,1,256,2048]{4,3,2,1,0:T(8,128)(2,1)S(1)} %slice_bitcast_fusion) | copy-start | bytes 3145732
  98.0 14.1 %collective-permute-start = (bf16[1,1,1,256,2048]{4,3,2,1,0:T(8,128)(2,1)S(1)}, bf16[1,1,1,256,2048]{4,3,2,1,0:T(8,128)(2,1)S(1)}, u32[]{:S(2)}, u32[]{:S(2)}) collective-permute-start(bf16[1,1,1,256,2048]{4,3,2,1,0:T(8,128)(2,1)S(1)} %slice_bitcast_fusion), channel_id=1, source_target_pairs={{0,64},{64,128},{128,192},{192,256},{256,320},{320,384},{384,448},... | collective-permute-start | bytes 3145736 | tf_op jit(solution)/shard_map/ppermute | solution.py:33
  100.4 16.1 %collective-permute-start.1 = (bf16[1,1,1,256,2048]{4,3,2,1,0:T(8,128)(2,1)S(1)}, bf16[1,1,1,256,2048]{4,3,2,1,0:T(8,128)(2,1)S(1)}, u32[]{:S(2)}, u32[]{:S(2)}) collective-permute-start(bf16[1,1,1,256,2048]{4,3,2,1,0:T(8,128)(2,1)S(1)} %slice_bitcast_fusion), channel_id=1, source_target_pairs={{64,0},{128,64},{192,128},{256,192},{320,256},{384,320},{448,384},... | collective-permute-start | bytes 3145736 | tf_op jit(solution)/shard_map/ppermute | solution.py:34
  112.1 135.5 %copy-start.4 = (bf16[1,1,1,256,2048]{4,3,2,1,0:T(8,128)(2,1)}, bf16[1,1,1,256,2048]{4,3,2,1,0:T(8,128)(2,1)S(1)}, u32[]{:S(2)}) copy-start(bf16[1,1,1,256,2048]{4,3,2,1,0:T(8,128)(2,1)S(1)} %collective-permute-done) | copy-start | bytes 3145732
  116.5 131.1 %copy-start.5 = (bf16[1,1,1,256,2048]{4,3,2,1,0:T(8,128)(2,1)}, bf16[1,1,1,256,2048]{4,3,2,1,0:T(8,128)(2,1)S(1)}, u32[]{:S(2)}) copy-start(bf16[1,1,1,256,2048]{4,3,2,1,0:T(8,128)(2,1)S(1)} %collective-permute-done.1) | copy-start | bytes 3145732
  118.5 130.9 %collective-permute-start.2 = (bf16[3,1,1,256,2048]{4,3,2,1,0:T(8,128)(2,1)}, bf16[3,1,1,256,2048]{4,3,2,1,0:T(8,128)(2,1)}, u32[]{:S(2)}, u32[]{:S(2)}) collective-permute-start(bf16[3,1,1,256,2048]{4,3,2,1,0:T(8,128)(2,1)} %pad_maximum_fusion.1), channel_id=1, source_target_pairs={{0,1},{1,2},{2,3},{3,4},{4,5},{5,6},{6,7},{7,8},{8,9},{9,10},{10,1... | collective-permute-start | bytes 9437192 | tf_op jit(solution)/shard_map/ppermute | solution.py:33
  123.9 125.6 %collective-permute-start.3 = (bf16[3,1,1,256,2048]{4,3,2,1,0:T(8,128)(2,1)}, bf16[3,1,1,256,2048]{4,3,2,1,0:T(8,128)(2,1)}, u32[]{:S(2)}, u32[]{:S(2)}) collective-permute-start(bf16[3,1,1,256,2048]{4,3,2,1,0:T(8,128)(2,1)} %pad_maximum_fusion.1), channel_id=1, source_target_pairs={{1,0},{2,1},{3,2},{4,3},{5,4},{6,5},{7,6},{8,7},{9,8},{10,9},{11,1... | collective-permute-start | bytes 9437192 | tf_op jit(solution)/shard_map/ppermute | solution.py:34
  259.0 86.5 %copy-start.3 = (bf16[1,1,1,256,1024]{4,3,2,1,0:T(8,128)(2,1)S(1)}, bf16[1,1,1,256,1024]{4,3,2,1,0:T(8,128)(2,1)}, u32[]{:S(2)}) copy-start(bf16[1,1,1,256,1024]{4,3,2,1,0:T(8,128)(2,1)} %param.7) | copy-start | bytes 1572868
  263.4 2.2 copy-start
  274.3 2.2 copy-start
  285.1 2.2 copy-start
  295.9 2.2 copy-start
  306.7 2.2 copy-start
  317.5 2.2 copy-start
  328.3 2.2 copy-start
  339.1 2.2 copy-start
Sparse Core Ops, SparseCore 0:
  48.5 43.5 all-gather.3
Sparse Core Ops, SparseCore 1:
  102.5 140.9 all-gather.5
where the time goes:
time: 357 us; the launch traced here: 356 us
  waiting for transfers between devices  175 us (49%)
  local copies, waits for them, and re-layouts  55.3 us (15%)
  matrix products  47.8 us (13%)
  blocking collectives  38.6 us (11%)
  between operations  15 us (4%)
  other arithmetic  12.3 us (3%)
  starting transfers between devices  11.1 us (3%)
    all_gather x1, waiting for transfers between devices, shards(): lax.all_gather(out_weight, ('region', 'owner'), axis=0, tiled=True)  118 us
    all_gather x1, waiting for transfers between devices, shards(): lax.all_gather(group_rows, 'region', axis=0, tiled=True)  43.2 us
    all_to_all x1, blocking collectives, from_everyone(): lax.all_to_all(jnp.broadcast_to(value[None], (devices, *value.shape)), ax...  38.6 us
    dot_general x8, matrix products, attend_group(): jnp.einsum('chsk,khd->cshd', attn_probs, value_part, preferred_element_ty...  26.1 us
    while x16, local copies, waits for them, and re-layouts  17.8 us
    dot_general x8, matrix products, attend_group(): jnp.einsum('cshd,khd->chsk', query_part, key_part, preferred_element_type...  13.9 us
    dynamic_slice x16, local copies, waits for them, and re-layouts, attend_group(): lax.dynamic_slice_in_dim(key_rows, offset, group_cols, 1)  12.8 us
    ppermute x2, waiting for transfers between devices, padded(): before = lax.ppermute(last, axis, up)  9.66 us
  transfers between devices with their start and end apart: 6, of which 4 were waited for; matrix products, arithmetic and copies ran while one was open for 2% of the time, Pallas kernels for 0%

commit v1 on v0

--- a/solution.py
+++ b/solution.py
@@ -54,7 +54,10 @@
     columns = normed
     qkv = jnp.dot(
         columns,
-        lax.all_gather(group_rows, "region", axis=0, tiled=True),
+        jnp.concatenate(
+            lax.all_to_all(jnp.stack([group_rows] * lax.axis_size("region")), "region", 0, 0),
+            axis=0,
+        ),
         preferred_element_type=jnp.float32,
     )
     qkv = qkv.astype(jnp.bfloat16)

time: 357 us -> 392 us (1.098)
  waiting for transfers between devices: 175 us -> 201 us
  starting transfers between devices: 11.1 us -> 18.7 us
    all_to_all x0 -> x1, waiting for transfers between devices: none -> 70.8 us  [shards(): lax.all_to_all(jnp.stack([group_rows] * lax.axis_size('region')), 'region...]
    all_gather x1 -> x0, waiting for transfers between devices: 43.2 us -> none  [shards(): lax.all_gather(group_rows, 'region', axis=0, tiled=True)]
    all_to_all x0 -> x1, starting transfers between devices: none -> 7.55 us  [shards(): lax.all_to_all(jnp.stack([group_rows] * lax.axis_size('region')), 'region...]
where the time goes in v1:
time: 392 us; the launch traced here: 390 us
  waiting for transfers between devices  201 us (51%)
  local copies, waits for them, and re-layouts  57.8 us (15%)
  matrix products  47.8 us (12%)
  blocking collectives  38.6 us (10%)
  starting transfers between devices  18.7 us (5%)
  between operations  13.5 us (3%)
  other arithmetic  12.3 us (3%)
    all_gather x1, waiting for transfers between devices, shards(): lax.all_gather(out_weight, ('region', 'owner'), axis=0, tiled=True)  116 us
    all_to_all x1, waiting for transfers between devices, shards(): lax.all_to_all(jnp.stack([group_rows] * lax.axis_size('region')), 'region...  70.8 us
    all_to_all x1, blocking collectives, from_everyone(): lax.all_to_all(jnp.broadcast_to(value[None], (devices, *value.shape)), ax...  38.6 us
    dot_general x8, matrix products, attend_group(): jnp.einsum('chsk,khd->cshd', attn_probs, value_part, preferred_element_ty...  26.1 us
    while x16, local copies, waits for them, and re-layouts  17.8 us
    dot_general x8, matrix products, attend_group(): jnp.einsum('cshd,khd->chsk', query_part, key_part, preferred_element_type...  13.9 us
    dynamic_slice x16, local copies, waits for them, and re-layouts, attend_group(): lax.dynamic_slice_in_dim(key_rows, offset, group_cols, 1)  12.8 us
    ppermute x2, waiting for transfers between devices, padded(): before = lax.ppermute(last, axis, up)  9.77 us
  transfers between devices with their start and end apart: 6, of which 4 were waited for; matrix products, arithmetic and copies ran while one was open for 2% of the time, Pallas kernels for 0%

profile of v1, /device:TPU:1, one launch (start us, length us, event | category | flops | bytes accessed | tf_op | source)
XLA Modules:
  0.0 390.5 jit_solution(2913370229700516287)
XLA Ops:
  7.7 38.6 %all_to_all.10 = bf16[64,2,3072]{2,1,0:T(2,128)(2,1)S(1)} all-to-all(bf16[64,2,3072]{2,1,0:T(2,128)(2,1)S(1)} %broadcast_in_dim.53), channel_id=1, replica_groups=mesh['region'=8,'owner'=64] {'owner'}, dimensions={0} | all-to-all | bytes 1572864 | tf_op jit(solution)/shard_map/all_to_all | solution.py:17
  46.6 3.4 stack.3
  50.0 7.6 %all-to-all-start.1 = ((bf16[8,128,3072]{2,1,0:T(8,128)(2,1)}), bf16[8,128,3072]{2,1,0:T(8,128)(2,1)}, u32[]{:S(2)}, u32[]{:S(2)}) async-start(bf16[8,128,3072]{2,1,0:T(8,128)(2,1)} %stack.3), calls=%async_computation.1 | async-start | bytes 12582912 | tf_op jit(solution)/shard_map/all_to_all | solution.py:58
  58.0 70.8 %all-to-all-done.1 = bf16[8,128,3072]{2,1,0:T(8,128)(2,1)} async-done(((bf16[8,128,3072]{2,1,0:T(8,128)(2,1)}), bf16[8,128,3072]{2,1,0:T(8,128)(2,1)}, u32[]{:S(2)}, u32[]{:S(2)}) %all-to-all-start.1) | async-done | bytes 6291488 | tf_op jit(solution)/shard_map/all_to_all | solution.py:58
  128.9 4.7 %convolution_convert_fusion = bf16[256,3072]{1,0:T(8,128)(2,1)S(1)} fusion(bf16[1024,3072]{1,0:T(8,128)(2,1)} %bitcast.2, bf16[1,1,1,256,1024]{4,3,2,1,0:T(8,128)(2,1)S(1)} %copy-done.2, f32[1024]{0:T(1024)S(1)} %copy-done.8, f32[256]{0:T(256)S(1)} %add_rsqrt_fusion, f32[256]{0:T(256)S(1)} %broadcast_multiply_fusion), kind=kOutput, calls=%fused_computation.17 | convolution fusion | flops 1612709888 | bytes 8394752 | tf_op jit(solution)/shard_map/dot_general | solution.py:55
  134.7 3.0 collective-permute-start
  139.7 9.8 %collective-permute-done = bf16[1,1,1,256,2048]{4,3,2,1,0:T(8,128)(2,1)S(1)} collective-permute-done((bf16[1,1,1,256,2048]{4,3,2,1,0:T(8,128)(2,1)S(1)}, bf16[1,1,1,256,2048]{4,3,2,1,0:T(8,128)(2,1)S(1)}, u32[]{:S(2)}, u32[]{:S(2)}) %collective-permute-start) | collective-permute-done | bytes 1048608 | tf_op jit(solution)/shard_map/ppermute | solution.py:33
  149.5 4.8 %collective-permute-done.1 = bf16[1,1,1,256,2048]{4,3,2,1,0:T(8,128)(2,1)S(1)} collective-permute-done((bf16[1,1,1,256,2048]{4,3,2,1,0:T(8,128)(2,1)S(1)}, bf16[1,1,1,256,2048]{4,3,2,1,0:T(8,128)(2,1)S(1)}, u32[]{:S(2)}, u32[]{:S(2)}) %collective-permute-start.1) | collective-permute-done | bytes 1048608 | tf_op jit(solution)/shard_map/ppermute | solution.py:34
  156.4 4.9 %collective-permute-start.2 = (bf16[3,1,1,256,2048]{4,3,2,1,0:T(8,128)(2,1)}, bf16[3,1,1,256,2048]{4,3,2,1,0:T(8,128)(2,1)}, u32[]{:S(2)}, u32[]{:S(2)}) collective-permute-start(bf16[3,1,1,256,2048]{4,3,2,1,0:T(8,128)(2,1)} %pad_maximum_fusion.1), channel_id=1, source_target_pairs={{0,1},{1,2},{2,3},{3,4},{4,5},{5,6},{6,7},{7,8},{8,9},{9,10},{10,1... | collective-permute-start | bytes 9437192 | tf_op jit(solution)/shard_map/ppermute | solution.py:33
  162.7 115.7 %all-gather.3.cloned.1.call-done = bf16[512,2,1024]{2,1,0:T(2,128)(2,1)} async-done(((bf16[1,2,1024]{2,1,0:T(2,128)(2,1)}), bf16[512,2,1024]{2,1,0:T(2,128)(2,1)}) %all-gather.3.cloned.1.call-update) | async-done | bytes 2097168 | tf_op jit(solution)/shard_map/all_gather | solution.py:123
  278.5 4.1 %reshape.323 = bf16[1024,1024]{1,0:T(8,128)(2,1)} reshape(bf16[512,2,1024]{2,1,0:T(2,128)(2,1)} %all-gather.3.cloned.1.call-done) | data formatting | bytes 4194304
  284.4 4.7 %pad_maximum_fusion = bf16[3,3,1,256,2048]{4,3,2,1,0:T(8,128)(2,1)S(1)} fusion(bf16[3,1,1,256,2048]{4,3,2,1,0:T(8,128)(2,1)} %collective-permute-done.3, bf16[1,1,1,256,2048]{4,3,2,1,0:T(8,128)(2,1)} %copy-done.5, bf16[1,1,1,256,2048]{4,3,2,1,0:T(8,128)(2,1)} %copy-done.1, bf16[1,1,1,256,2048]{4,3,2,1,0:T(8,128)(2,1)} %copy-done.4, ...), kind=kLoop, calls=%fused_computation.16 | loop fusion | flops 18874368 | bytes 18874368 | tf_op jit(solution)/shard_map/concatenate | solution.py:35
  289.1 4.8 %fusion.29 = (bf16[2304,1024]{1,0:T(8,128)(2,1)}, bf16[2304,1024]{1,0:T(8,128)(2,1)}) fusion(bf16[2304,2048]{1,0:T(8,128)(2,1)S(1)} %bitcast.102), kind=kLoop, calls=%fused_computation.53 | loop fusion | bytes 18874368 | tf_op jit(solution)/shard_map/slice | solution.py:68
  293.9 86.6 %while.14 = (s32[]{:T(128)}, bf16[1,256,1024]{1,2,0:T(8,128)(2,1)S(1)}, bf16[2304,1024]{1,0:T(8,128)(2,1)}, bf16[2304,1024]{1,0:T(8,128)(2,1)}, bf16[1,256,1024]...) while((s32[]{:T(128)}, ...), condition=%wide.region_6.7_spmd.clone, body=%wide.region_3.6_spmd.clone.sunk | while | flops 311458816 | bytes 39472324 | solution.py:116
  298.4 2.2 copy-done
  301.5 3.3 fusion.46
  312.3 3.3 fusion.46
  323.1 3.3 fusion.46
  333.9 3.3 fusion.46
  344.7 3.3 fusion.46
  355.6 3.3 fusion.46
  366.4 3.3 fusion.46
  377.2 3.3 fusion.46
  380.5 3.1 fusion.13
  (130 shorter events, 68.1 us)
Async XLA Ops:
  50.0 7.6 %copy-start.2 = (bf16[1,1,1,256,1024]{4,3,2,1,0:T(8,128)(2,1)S(1)}, bf16[1,1,1,256,1024]{4,3,2,1,0:T(8,128)(2,1)}, u32[]{:S(2)}) copy-start(bf16[1,1,1,256,1024]{4,3,2,1,0:T(8,128)(2,1)} %param.7) | copy-start | bytes 1572868
  50.0 78.8 %copy-start.8 = (f32[1024]{0:T(1024)S(1)}, f32[1024]{0:T(1024)}, u32[]{:S(2)}) copy-start(f32[1024]{0:T(1024)} %param.8) | copy-start | bytes 12292
  50.0 78.8 %all-to-all-start.1 = ((bf16[8,128,3072]{2,1,0:T(8,128)(2,1)}), bf16[8,128,3072]{2,1,0:T(8,128)(2,1)}, u32[]{:S(2)}, u32[]{:S(2)}) async-start(bf16[8,128,3072]{2,1,0:T(8,128)(2,1)} %stack.3), calls=%async_computation.1 | async-start | bytes 12582912 | tf_op jit(solution)/shard_map/all_to_all | solution.py:58
  57.6 220.9 %all-gather.3.cloned.1.call-start = ((), (), s32[]{:S(2)}) async-start(), calls=%async_computation.2 | async-start | bytes 2101248 | tf_op jit(solution)/shard_map/all_gather | solution.py:123
  133.5 1.2 copy-start.6
  133.6 29.0 %copy-start.7 = (s32[1,1,1,8]{3,2,1,0:T(1,128)S(1)}, s32[1,1,1,8]{3,2,1,0:T(1,128)}, u32[]{:S(2)}) copy-start(s32[1,1,1,8]{3,2,1,0:T(1,128)} %param.11) | copy-start | bytes 100
  134.7 147.8 %copy-start.1 = (bf16[1,1,1,256,2048]{4,3,2,1,0:T(8,128)(2,1)}, bf16[1,1,1,256,2048]{4,3,2,1,0:T(8,128)(2,1)S(1)}, u32[]{:S(2)}) copy-start(bf16[1,1,1,256,2048]{4,3,2,1,0:T(8,128)(2,1)S(1)} %slice_bitcast_fusion) | copy-start | bytes 3145732
  134.7 14.8 %collective-permute-start = (bf16[1,1,1,256,2048]{4,3,2,1,0:T(8,128)(2,1)S(1)}, bf16[1,1,1,256,2048]{4,3,2,1,0:T(8,128)(2,1)S(1)}, u32[]{:S(2)}, u32[]{:S(2)}) collective-permute-start(bf16[1,1,1,256,2048]{4,3,2,1,0:T(8,128)(2,1)S(1)} %slice_bitcast_fusion), channel_id=1, source_target_pairs={{0,64},{64,128},{128,192},{192,256},{256,320},{320,384},{384,448},... | collective-permute-start | bytes 3145736 | tf_op jit(solution)/shard_map/ppermute | solution.py:33
  137.8 16.5 %collective-permute-start.1 = (bf16[1,1,1,256,2048]{4,3,2,1,0:T(8,128)(2,1)S(1)}, bf16[1,1,1,256,2048]{4,3,2,1,0:T(8,128)(2,1)S(1)}, u32[]{:S(2)}, u32[]{:S(2)}) collective-permute-start(bf16[1,1,1,256,2048]{4,3,2,1,0:T(8,128)(2,1)S(1)} %slice_bitcast_fusion), channel_id=1, source_target_pairs={{64,0},{128,64},{192,128},{256,192},{320,256},{384,320},{448,384},... | collective-permute-start | bytes 3145736 | tf_op jit(solution)/shard_map/ppermute | solution.py:34
  149.5 133.0 %copy-start.4 = (bf16[1,1,1,256,2048]{4,3,2,1,0:T(8,128)(2,1)}, bf16[1,1,1,256,2048]{4,3,2,1,0:T(8,128)(2,1)S(1)}, u32[]{:S(2)}) copy-start(bf16[1,1,1,256,2048]{4,3,2,1,0:T(8,128)(2,1)S(1)} %collective-permute-done) | copy-start | bytes 3145732
  154.3 128.2 %copy-start.5 = (bf16[1,1,1,256,2048]{4,3,2,1,0:T(8,128)(2,1)}, bf16[1,1,1,256,2048]{4,3,2,1,0:T(8,128)(2,1)S(1)}, u32[]{:S(2)}) copy-start(bf16[1,1,1,256,2048]{4,3,2,1,0:T(8,128)(2,1)S(1)} %collective-permute-done.1) | copy-start | bytes 3145732
  156.4 128.1 %collective-permute-start.2 = (bf16[3,1,1,256,2048]{4,3,2,1,0:T(8,128)(2,1)}, bf16[3,1,1,256,2048]{4,3,2,1,0:T(8,128)(2,1)}, u32[]{:S(2)}, u32[]{:S(2)}) collective-permute-start(bf16[3,1,1,256,2048]{4,3,2,1,0:T(8,128)(2,1)} %pad_maximum_fusion.1), channel_id=1, source_target_pairs={{0,1},{1,2},{2,3},{3,4},{4,5},{5,6},{6,7},{7,8},{8,9},{9,10},{10,1... | collective-permute-start | bytes 9437192 | tf_op jit(solution)/shard_map/ppermute | solution.py:33
  161.3 123.1 %collective-permute-start.3 = (bf16[3,1,1,256,2048]{4,3,2,1,0:T(8,128)(2,1)}, bf16[3,1,1,256,2048]{4,3,2,1,0:T(8,128)(2,1)}, u32[]{:S(2)}, u32[]{:S(2)}) collective-permute-start(bf16[3,1,1,256,2048]{4,3,2,1,0:T(8,128)(2,1)} %pad_maximum_fusion.1), channel_id=1, source_target_pairs={{1,0},{2,1},{3,2},{4,3},{5,4},{6,5},{7,6},{8,7},{9,8},{10,9},{11,1... | collective-permute-start | bytes 9437192 | tf_op jit(solution)/shard_map/ppermute | solution.py:34
  293.9 86.6 %copy-start.3 = (bf16[1,1,1,256,1024]{4,3,2,1,0:T(8,128)(2,1)S(1)}, bf16[1,1,1,256,1024]{4,3,2,1,0:T(8,128)(2,1)}, u32[]{:S(2)}) copy-start(bf16[1,1,1,256,1024]{4,3,2,1,0:T(8,128)(2,1)} %param.7) | copy-start | bytes 1572868
  298.4 2.2 copy-start
  309.2 2.2 copy-start
  320.0 2.2 copy-start
  330.8 2.2 copy-start
  341.6 2.2 copy-start
  352.4 2.2 copy-start
  363.3 2.2 copy-start
  374.1 2.2 copy-start
Sparse Core Ops, SparseCore 0:
  139.9 138.5 all-gather.2
